TPU v7x, 32 devices: a whole 2x2x4 slice. The times are simulated.
32 devices in a mesh: grp: 2 (over x), gx: 16 (over z, y, core).
Axes of the slice: x: 2, y: 2, z: 4, core: 2. Of those that a mesh axis runs over, the one named last changes fastest.
Arguments:
- voltages: bfloat16 [1024, 143360], P(('grp', 'gx')), parts along dimension 0, may hold values from -6 to 6
- taps: float32 [4, 4096], replicated, may hold values from -3 to 3
- weights: bfloat16 [2, 64, 256, 128], P(None, 'gx'), may hold values from -0.25 to 0.25
- antenna_weight_index: int32 [1024], P(('grp', 'gx')), parts along dimension 0, may hold values from 0 to 255
- flagged: int32 [1024], P(('grp', 'gx')), parts along dimension 0, may hold values 0 or 1
- trials: int32 [256], P(('grp', 'gx')), parts along dimension 0, may hold values from 0 to 63
Outputs:
- dedispersed: float32 [2, 32, 256, 64], P(None, None, ('grp', 'gx')), parts along dimension 2
There are 2 independent parts, one for each index of `grp`. A program takes and returns all parts, laid end to end along the dimension named above; an argument that names none is the same for every part. Nothing has to cross between parts.
All inputs are finite; a program needn't handle non-finite values. No bound on the sum of `flagged` on one device may be relied on, other than what follows from the above.
Results may differ from a plain program's by a relative error of at most 0.009.
Values may be sent and summed in bfloat16 or wider, within the bound.
A program may use at most 64 MiB of HBM per device.

v0:
```python
import functools
import math

import jax
import jax.numpy as jnp
import numpy as np
from jax import lax
from jax.experimental import pallas as pl
from jax.experimental.pallas import tpu as pltpu
from jax.sharding import PartitionSpec as P

FRAME_COUNT = 32
FORWARD_LENGTH = 4096
TAP_COUNT = 4
CH_LO = 1024
WEIGHT_ROWS = 256
LANES = 128
DM_UNIT = 0.173
MESH = pl.DeviceIdType.MESH
NT = (((1,), (1,)), ((), ()))


def twiddles(channels, owners):
    local = channels // owners
    kept = (np.arange(owners)[:, None, None] * local + np.arange(local)[None, None, :]) + np.zeros((1, 2, 1), np.int64)
    part = np.zeros((owners, 1, local), np.int64) + np.arange(2)[None, :, None]
    kept, part = kept.reshape(-1, 1), part.reshape(-1, 1)
    coarse = (CH_LO + kept) * (np.arange(FORWARD_LENGTH // LANES) * LANES)[None] % FORWARD_LENGTH
    fine = (CH_LO + kept) * np.arange(LANES)[None] % FORWARD_LENGTH
    unit = 2.0 * math.pi / FORWARD_LENGTH
    ch, sh = np.cos(coarse * unit), np.sin(coarse * unit)
    first = np.where(part == 0, ch, -sh)
    second = np.where(part == 0, -sh, -ch)
    pad = np.zeros((first.shape[0], LANES - 2 * first.shape[1]))
    return (
        np.concatenate([first, second, pad], 1).astype(np.float32),
        np.stack([np.cos(fine * unit), np.sin(fine * unit)]).astype(np.float32),
    )


def inverse_rows(channels, owners):
    local = channels // owners
    chan = (np.arange(owners)[None, :] * local + np.arange(local)[:, None])[:, None, :, None]
    time = np.arange(channels)[None, None, None, :]
    angle = (chan * time % channels) * (2.0 * math.pi / channels)
    cosine, sine = np.cos(angle), np.sin(angle)
    real = np.concatenate([cosine, -sine], 1)
    imag = np.concatenate([sine, cosine], 1)
    return np.stack([real, imag]).reshape(2, 2 * channels, channels).astype(jnp.bfloat16)


GROUPS = (8, 8, 8, 8, 3)


def kernel(
    n, plan, index, flagged, trials, volts_hbm, taps, coarse, fine, weights_hbm, inverse, out,
    volts, weights, table, tapped, keep, chirp, index_row, spec,
    got_index, got_spec, gathered, lined, sending, got_beams, turned, stacked,
    load_sems, send_sems, index_sems, spec_sems, beam_sems,
):
    me = lax.axis_index("gx")
    rows = coarse.shape[0]
    antennas = volts.shape[0]
    locals_ = weights.shape[1]
    beam_total = weights.shape[3]
    channels = n * locals_
    frames = FRAME_COUNT
    quad = LANES // antennas
    parts = 2 * locals_
    beams = sending.shape[1] // 2
    steps = len(plan)

    loads = []
    for at in range(steps):
        span = pl.ds(sum(GROUPS[:at]) * FORWARD_LENGTH, GROUPS[at] * FORWARD_LENGTH)
        loads.append(pltpu.make_async_copy(volts_hbm.at[:, span], volts.at[:, span], load_sems.at[at]))
    loads.append(pltpu.make_async_copy(weights_hbm, weights, load_sems.at[steps]))
    for load in loads[:2]:
        load.start()

    barrier = pltpu.get_barrier_semaphore()
    for d in range(1, n):
        pl.semaphore_signal(barrier, inc=1, device_id={"gx": lax.rem(me + d, n)}, device_id_type=MESH)

    lane_one = lax.broadcasted_iota(jnp.int32, (1, LANES), 1) % antennas
    row = jnp.zeros((1, LANES), jnp.int32)
    for a in range(antennas):
        row = jnp.where(lane_one == a, index[a], row)
    index_row[...] = row
    antenna = lax.broadcasted_iota(jnp.int32, (antennas, LANES), 0)
    off = jnp.zeros((antennas, LANES), jnp.int32)
    for a in range(antennas):
        off = jnp.where(antenna == a, flagged[a], off)
    keep[...] = (1 - off).astype(jnp.float32) * FORWARD_LENGTH ** (-0.5)

    def copies(which, source, target, sems):
        made = []
        for d in range(1, n):
            peer = lax.rem(me + d, n)
            made.append(
                pltpu.make_async_remote_copy(
                    src_ref=source(peer),
                    dst_ref=target(me),
                    send_sem=send_sems.at[which, d],
                    recv_sem=sems.at[d],
                    device_id={"gx": peer},
                    device_id_type=MESH,
                )
            )
        for copy in made:
            copy.start()
        return made

    def arrivals(which, source, target, sems):
        for d in range(1, n):
            peer = lax.rem(me + n - d, n)
            pltpu.make_async_remote_copy(
                src_ref=source(peer),
                dst_ref=target(peer),
                send_sem=send_sems.at[which, d],
                recv_sem=sems.at[d],
                device_id={"gx": peer},
                device_id_type=MESH,
            ).wait_recv()

    index_args = (steps, lambda p: index_row, lambda p: got_index.at[p], index_sems)
    beam_args = (steps + 1, lambda p: sending.at[p], lambda p: got_beams.at[p], beam_sems)

    def piece_args(at):
        span = pl.ds(plan[at][0] * LANES, (plan[at][1] - plan[at][0]) * LANES)
        return (at, lambda p: spec.at[p, :, span], lambda p: got_spec.at[p, :, span], spec_sems.at[at])

    half = FORWARD_LENGTH // LANES
    for tile in range(half):
        span = slice(tile * LANES, (tile + 1) * LANES)
        base = (
            coarse[:, tile : tile + 1] * fine[0]
            + coarse[:, half + tile : half + tile + 1] * fine[1]
        )
        for tap in range(TAP_COUNT):
            table[tap * rows : (tap + 1) * rows, span] = (base * taps[tap : tap + 1, span]).astype(jnp.bfloat16)

    started = []

    def emit(tile):
        for part in range(rows // LANES):
            pieces = []
            for f in range(tile * quad, (tile + 1) * quad):
                total = None
                for tap in range(TAP_COUNT):
                    term = tapped[
                        (f + tap) * antennas : (f + tap + 1) * antennas,
                        tap * rows + part * LANES : tap * rows + (part + 1) * LANES,
                    ]
                    total = term if total is None else total + term
                pieces.append(total * keep[...])
            across = jnp.concatenate(pieces, 0).T
            eights = LANES // parts
            spec[part * eights : (part + 1) * eights, :, tile * LANES : (tile + 1) * LANES] = across.reshape(
                eights, parts, LANES
            ).astype(jnp.bfloat16)

    def gather_weights():
        arrivals(*index_args)
        loads[steps].wait()
        lane = lax.broadcasted_iota(jnp.int32, (LANES, LANES), 1)
        lane_quad = lax.broadcasted_iota(jnp.int32, (1, LANES), 1) // antennas
        for ag in range(n // quad):
            row = got_index[ag * quad]
            for q in range(1, quad):
                row = jnp.where(lane_quad == q, got_index[ag * quad + q], row)
            column = jnp.broadcast_to(row.astype(jnp.float32), (LANES, LANES)).T
            column = column.astype(jnp.int32)
            onehot = jnp.concatenate(
                [
                    jnp.where(column == lane + t * LANES, 1.0, 0.0).astype(jnp.bfloat16)
                    for t in range(WEIGHT_ROWS // LANES)
                ],
                1,
            )
            for c in range(locals_):
                for r in range(2):
                    gathered[
                        c, ag * LANES : (ag + 1) * LANES, r * beam_total : (r + 1) * beam_total
                    ] = jnp.dot(onehot, weights[r, c], preferred_element_type=jnp.float32).astype(jnp.bfloat16)

    def turn():
        beam = lax.broadcasted_iota(jnp.int32, (beams, LANES), 0)
        trial = jnp.zeros((beams, LANES), jnp.int32)
        for b in range(beams):
            trial = jnp.where(beam == b, trials[b], trial)
        scaled = (-2.0 * math.pi * DM_UNIT) * (trial.astype(jnp.float32) + 1.0)
        lane_chan = lax.broadcasted_iota(jnp.int32, (n, beams, LANES), 2) // frames
        owner = lax.broadcasted_iota(jnp.int32, (n, beams, LANES), 0)
        chan = (owner * locals_ + lane_chan).astype(jnp.float32) / channels
        phase = scaled[None] * (chan * chan)
        chirp[0] = jnp.cos(phase)
        chirp[1] = jnp.sin(phase)

    for at in range(steps):
        loads[at].wait()
        if at + 2 < len(loads):
            loads[at + 2].start()
        begin = sum(GROUPS[:at])
        left = jnp.concatenate(
            [volts[:, g * FORWARD_LENGTH : (g + 1) * FORWARD_LENGTH] for g in range(begin, begin + GROUPS[at])], 0
        )
        tapped[begin * antennas : (begin + GROUPS[at]) * antennas, :] = lax.dot_general(
            left, table[...], NT, preferred_element_type=jnp.float32
        )
        for tile in range(*plan[at]):
            emit(tile)
        if at == 0:
            pl.semaphore_wait(barrier, n - 1)
            started += copies(*index_args)
            got_index[me] = index_row[...]
        started += copies(*piece_args(at))
        if at == steps - 2:
            gather_weights()
        if at == steps - 3:
            turn()
    got_spec[me] = spec[me]

    lane_part = lax.broadcasted_iota(jnp.int32, (parts, LANES), 1) // antennas
    for at in range(steps):
        arrivals(*piece_args(at))
        for sg in range(n // quad):
            for ft in range(*plan[at]):
                pieces = [
                    got_spec[sg * quad + s, :, ft * LANES : (ft + 1) * LANES].astype(jnp.float32)
                    for s in range(quad)
                ]
                for f in range(quad):
                    made = None
                    for s in range(quad):
                        piece = pieces[s]
                        if s != f:
                            piece = pltpu.roll(piece, ((s - f) * antennas) % LANES, 1)
                        made = piece if made is None else jnp.where(lane_part == s, piece, made)
                    to = (ft * quad + f) * parts
                    lined[sg, to : to + parts, :] = made

    real, imag = [], []
    for c in range(locals_):
        left = jnp.concatenate(
            [
                jnp.concatenate(
                    [lined[sg, pl.ds(r * locals_ + c, frames, stride=parts), :] for sg in range(n // quad)], 1
                )
                for r in range(2)
            ],
            0,
        ).astype(jnp.bfloat16)
        both = jnp.dot(left, gathered[c], preferred_element_type=jnp.float32)
        real.append(both[:frames, :beam_total] - both[frames:, beam_total:])
        imag.append(both[:frames, beam_total:] + both[frames:, :beam_total])
    real, imag = jnp.concatenate(real, 0), jnp.concatenate(imag, 0)
    owners = LANES // beams
    for bt in range(beam_total // LANES):
        span = slice(bt * LANES, (bt + 1) * LANES)
        pair = [x[:, span].T.reshape(owners, beams, LANES) for x in (real, imag)]
        sending[bt * owners : (bt + 1) * owners] = jnp.concatenate(pair, 1).astype(jnp.bfloat16)

    started += copies(*beam_args)
    got_beams[me] = sending[me]
    arrivals(*beam_args)

    for s in range(n):
        block = got_beams[s].astype(jnp.float32)
        x, y = block[:beams], block[beams:]
        cosine, sine = chirp[0, s], chirp[1, s]
        turned[pl.ds(s, beams, stride=2 * n), :] = x * cosine - y * sine
        turned[pl.ds(n + s, beams, stride=2 * n), :] = x * sine + y * cosine

    wide = 2 * n
    deep = locals_ * wide // LANES
    if wide >= LANES:
        for b in range(beams):
            for t in range(wide // LANES):
                across = turned[b * wide + t * LANES : b * wide + (t + 1) * LANES, :].T
                for c in range(locals_):
                    stacked[c * (wide // LANES) + t, pl.ds(b, frames, stride=beams), :] = across[
                        c * frames : (c + 1) * frames
                    ]
    else:
        each = LANES // wide
        place = lax.broadcasted_iota(jnp.int32, (frames, LANES), 1) // wide
        for g in range(beams // each):
            across = turned[g * LANES : (g + 1) * LANES, :].T
            for b in range(each):
                for k in range(deep):
                    made = None
                    for slot in range(each):
                        c = k * each + slot
                        piece = across[c * frames : (c + 1) * frames]
                        if b != slot:
                            piece = pltpu.roll(piece, ((slot - b) * wide) % LANES, 1)
                        made = piece if made is None else jnp.where(place == slot, piece, made)
                    stacked[k, pl.ds(g * each + b, frames, stride=beams), :] = made
    left = jnp.concatenate([stacked[k] for k in range(deep)], 1).astype(jnp.bfloat16)
    for s in range(2):
        total = jnp.dot(left, inverse[s], preferred_element_type=jnp.float32) * channels ** (-0.5)
        out[s] = total.reshape(frames, beams, channels)

    for copy in started:
        copy.wait_send()


def per_device(voltages, taps, weights, antenna_weight_index, flagged, trials):
    n = lax.axis_size("gx")
    locals_ = weights.shape[1]
    beam_total = weights.shape[3]
    channels = locals_ * n
    antennas = voltages.shape[0]
    beams = trials.shape[0]
    parts = 2 * locals_
    rows = 2 * channels
    total = FRAME_COUNT + TAP_COUNT - 1
    steps = len(GROUPS)
    coarse, fine = twiddles(channels, n)
    inverse = inverse_rows(channels, n)
    quad = LANES // antennas
    plan, ready = [], 0
    for at in range(steps):
        done = (sum(GROUPS[: at + 1]) - TAP_COUNT + 1) // quad
        plan.append((ready, done))
        ready = done
    vmem = pl.BlockSpec(memory_space=pltpu.VMEM)
    smem = pl.BlockSpec(memory_space=pltpu.SMEM)
    hbm = pl.BlockSpec(memory_space=pltpu.HBM)
    return pl.pallas_call(
        functools.partial(kernel, n, plan),
        out_shape=jax.ShapeDtypeStruct((2, FRAME_COUNT, beams, channels), jnp.float32),
        in_specs=[smem, smem, smem, hbm, vmem, vmem, vmem, hbm, vmem],
        out_specs=vmem,
        scratch_shapes=[
            pltpu.VMEM(voltages.shape, jnp.bfloat16),
            pltpu.VMEM(weights.shape, jnp.bfloat16),
            pltpu.VMEM((TAP_COUNT * rows, FORWARD_LENGTH), jnp.bfloat16),
            pltpu.VMEM((total * antennas, TAP_COUNT * rows), jnp.float32),
            pltpu.VMEM((antennas, LANES), jnp.float32),
            pltpu.VMEM((2, n, beams, LANES), jnp.float32),
            pltpu.VMEM((1, LANES), jnp.int32),
            pltpu.VMEM((n, parts, FRAME_COUNT * antennas), jnp.bfloat16),
            pltpu.VMEM((n, 1, LANES), jnp.int32),
            pltpu.VMEM((n, parts, FRAME_COUNT * antennas), jnp.bfloat16),
            pltpu.VMEM((locals_, n * antennas, 2 * beam_total), jnp.bfloat16),
            pltpu.VMEM((n * antennas // LANES, FRAME_COUNT * parts, LANES), jnp.float32),
            pltpu.VMEM((n, 2 * beams, LANES), jnp.bfloat16),
            pltpu.VMEM((n, 2 * beams, LANES), jnp.bfloat16),
            pltpu.VMEM((beams * 2 * n, LANES), jnp.float32),
            pltpu.VMEM((2 * channels // LANES, FRAME_COUNT * beams, LANES), jnp.float32),
            pltpu.SemaphoreType.DMA((steps + 1,)),
            pltpu.SemaphoreType.DMA((steps + 2, n)),
            pltpu.SemaphoreType.DMA((n,)),
            pltpu.SemaphoreType.DMA((steps, n)),
            pltpu.SemaphoreType.DMA((n,)),
        ],
        compiler_params=pltpu.CompilerParams(collective_id=0, has_side_effects=True, vmem_limit_bytes=67043328),
        name="beamformer",
    )(
        antenna_weight_index, flagged, trials, voltages, taps,
        jnp.asarray(coarse), jnp.asarray(fine), weights, jnp.asarray(inverse),
    )


def solution(mesh):
    return jax.shard_map(
        per_device,
        mesh=mesh,
        in_specs=(
            P(("grp", "gx"), None),
            P(),
            P(None, "gx", None, None),
            P(("grp", "gx")),
            P(("grp", "gx")),
            P(("grp", "gx")),
        ),
        out_specs=P(None, None, ("grp", "gx"), None),
        check_vma=False,
    )
```

profile of v0, /device:TPU:0, one launch (start us, length us, event | category | flops | bytes accessed | tf_op | source)
XLA Modules:
  0.0 27.6 jit_solution(2251534225790388976)
XLA Ops:
  0.0 25.9 %beamformer.1 = f32[2,32,8,64]{3,2,1,0:T(8,128)} custom-call(s32[32]{0:T(128)} %index.1, s32[32]{0:T(128)} %flagged.1, s32[8]{0:T(128)} %trials.1, bf16[32,143360]{1,0:T(8,128)(2,1)} %volts_hbm.1, f32[4,4096]{1,0:T(4,128)} %taps.1, f32[128,128]{1,0:T(8,128)} %constant.6.clone.coarse, f32[2,128,128]{2,1,0:T(8,128)} %constant.7.clone.fine, ...), custom_call_target="tpu_custom_call" | custom-call | tf_op jit(solution)/shard_map/beamformer/pallas_call | solution.py:331
  25.9 1.7 %copy.11 = f32[2,32,8,64]{3,2,1,0:T(8,128)} copy(f32[2,32,8,64]{3,2,1,0:T(8,128)} %beamformer.1) | data formatting | bytes 262144
where the time goes:
time: 27.7 us; the launch traced here: 27.6 us
  Pallas kernels  25.9 us (94%)
  local copies, waits for them, and re-layouts  1.67 us (6%)
    pallas_call x1, Pallas kernels, per_device(): pl.pallas_call(functools.partial(kernel, n, plan), out_shape=jax.ShapeDty...  25.9 us
    unnamed x1, local copies, waits for them, and re-layouts  1.67 us

commit v1 on v0

v1 whole, which is shorter than its diff:
```python
import functools
import math

import jax
import jax.numpy as jnp
import numpy as np
from jax import lax
from jax.experimental import pallas as pl
from jax.experimental.pallas import tpu as pltpu
from jax.sharding import PartitionSpec as P

FRAME_COUNT = 32
FORWARD_LENGTH = 4096
TAP_COUNT = 4
CH_LO = 1024
WEIGHT_ROWS = 256
LANES = 128
SUBLANES = 16
DM_UNIT = 0.173
MESH = pl.DeviceIdType.MESH
VMEM_BYTES = 67108864
GROUPS = (8, 8, 8, 8)
K_TILE = 256


def forward_columns(channels, owners):
    local = channels // owners
    kept = np.arange(channels).reshape(owners, 1, local)
    bins = np.broadcast_to(CH_LO + kept, (owners, 2, local)).reshape(-1)
    part = np.broadcast_to(np.arange(2).reshape(1, 2, 1), (owners, 2, local)).reshape(-1)
    angle = (np.arange(FORWARD_LENGTH)[:, None] * bins[None] % FORWARD_LENGTH) * (2.0 * math.pi / FORWARD_LENGTH)
    return np.where(part[None] == 0, np.cos(angle), -np.sin(angle)).astype(jnp.bfloat16)


def inverse_rows(channels, owners):
    local = channels // owners
    chan = (np.arange(owners)[None, :] * local + np.arange(local)[:, None]).reshape(1, -1, 1)
    angle = (chan * np.arange(channels) % channels) * (2.0 * math.pi / channels)
    cosine, sine = np.cos(angle), np.sin(angle)
    real = np.concatenate([cosine, -sine], 0)
    imag = np.concatenate([sine, cosine], 0)
    return np.stack([real, imag]).reshape(2, 2 * channels, channels).astype(jnp.bfloat16)


def kernel(
    n, index_hbm, flagged_hbm, trials_hbm, volts_hbm, taps_hbm, table_hbm, weights_hbm, inverse_hbm, out,
    index, flagged, trials, volts, taps, table, weights, inverse,
    wide_taps, keep, chirp, index_rows, spec,
    got_index, got_spec, gathered, lined, sending, got_beams, turned, stacked,
    load_sems, remote_sems,
):
    me = lax.axis_index("gx")
    antennas = volts.shape[0]
    locals_ = weights.shape[1]
    beam_total = weights.shape[3]
    channels = n * locals_
    rows = 2 * channels
    frames = FRAME_COUNT
    quad = LANES // antennas
    parts = 2 * locals_
    half = LANES // parts
    halves = frames // half
    beams = beam_total // n
    steps = len(GROUPS)

    barrier = pltpu.get_barrier_semaphore()
    for d in range(1, n):
        pl.semaphore_signal(barrier, inc=1, device_id={"gx": lax.rem(me + d, n)}, device_id_type=MESH)

    def load(source, target, at):
        return pltpu.make_async_copy(source, target, load_sems.at[at])

    streams = []
    for at in range(steps):
        begin = sum(GROUPS[:at]) + (TAP_COUNT - 1 if at else 0)
        end = sum(GROUPS[: at + 1]) + TAP_COUNT - 1
        span = pl.ds(begin * FORWARD_LENGTH, (end - begin) * FORWARD_LENGTH)
        streams.append(load(volts_hbm.at[:, span], volts.at[:, span], at))
    load_taps = load(taps_hbm, taps, steps)
    load_table = load(table_hbm, table, steps + 1)
    load_weights = load(weights_hbm, weights, steps + 2)
    load_inverse = load(inverse_hbm, inverse, steps + 3)
    load_index = load(index_hbm, index, steps + 4)
    load_flagged = load(flagged_hbm, flagged, steps + 5)
    load_trials = load(trials_hbm, trials, steps + 6)
    for one in (load_taps, load_table, streams[0], load_index, load_flagged, load_trials):
        one.start()
    streams[1].start()

    def copies(source, target, send, recv):
        for d in range(1, n):
            peer = lax.rem(me + d, n)
            pltpu.make_async_remote_copy(
                src_ref=source(peer),
                dst_ref=target(me),
                send_sem=send,
                recv_sem=recv,
                device_id={"gx": peer},
                device_id_type=MESH,
            ).start()

    def whole(source, target, send, recv):
        others = pl.ds(0, n - 1)
        return pltpu.make_async_remote_copy(
            src_ref=source(others),
            dst_ref=target(others),
            send_sem=send,
            recv_sem=recv,
            device_id={"gx": lax.rem(me + 1, n)},
            device_id_type=MESH,
        )

    index_args = (lambda p: index_rows.at[p], lambda p: got_index.at[p], remote_sems.at[0], remote_sems.at[1])

    def spans(at):
        return sum(GROUPS[:at]) // quad, sum(GROUPS[: at + 1]) // quad

    def piece_args(at):
        first, last = spans(at)
        span = pl.ds(first * LANES, (last - first) * LANES)
        return (
            lambda p: spec.at[p, :, span], lambda p: got_spec.at[p, :, span],
            remote_sems.at[2 + 2 * at], remote_sems.at[3 + 2 * at],
        )

    def beam_args(h):
        return (
            lambda p: sending.at[h, p], lambda p: got_beams.at[h, p],
            remote_sems.at[2 + 2 * (steps + h)], remote_sems.at[3 + 2 * (steps + h)],
        )

    load_taps.wait()
    for tap in range(TAP_COUNT):
        wide_taps[tap] = jnp.broadcast_to(taps[tap : tap + 1, :], (SUBLANES, FORWARD_LENGTH)).astype(jnp.bfloat16)

    def filtered(at, k):
        span = slice(k * K_TILE, (k + 1) * K_TILE)
        tap = [wide_taps[j, :, span] for j in range(TAP_COUNT)]
        first = sum(GROUPS[:at])
        pieces = []
        for block in range(antennas // SUBLANES):
            x = [
                volts[
                    block * SUBLANES : (block + 1) * SUBLANES,
                    f * FORWARD_LENGTH + k * K_TILE : f * FORWARD_LENGTH + (k + 1) * K_TILE,
                ]
                for f in range(first, first + GROUPS[at] + TAP_COUNT - 1)
            ]
            pieces.append(
                [
                    (x[f] * tap[0] + x[f + 1] * tap[1]) + (x[f + 2] * tap[2] + x[f + 3] * tap[3])
                    for f in range(GROUPS[at])
                ]
            )
        return jnp.concatenate([piece[f] for f in range(GROUPS[at]) for piece in pieces], 0)

    def emit(at, total):
        first, last = spans(at)
        eights = LANES // parts
        for tile in range(first, last):
            block = total[(tile - first) * LANES : (tile - first + 1) * LANES]
            for part in range(rows // LANES):
                across = (block[:, part * LANES : (part + 1) * LANES] * keep[...]).T
                spec[part * eights : (part + 1) * eights, :, tile * LANES : (tile + 1) * LANES] = across.reshape(
                    eights, parts, LANES
                ).astype(jnp.bfloat16)

    def small():
        load_index.wait()
        load_flagged.wait()
        lane_one = lax.broadcasted_iota(jnp.int32, (1, LANES), 1) % antennas
        row = jnp.zeros((1, LANES), jnp.int32)
        for a in range(antennas):
            row = jnp.where(lane_one == a, index[a], row)
        index_rows[...] = jnp.broadcast_to(row[None], index_rows.shape)
        antenna = lax.broadcasted_iota(jnp.int32, (antennas, LANES), 0)
        off = jnp.zeros((antennas, LANES), jnp.int32)
        for a in range(antennas):
            off = jnp.where(antenna == a, flagged[a], off)
        kept = (1 - off).astype(jnp.float32) * FORWARD_LENGTH ** (-0.5)
        for q in range(quad):
            keep[q * antennas : (q + 1) * antennas, :] = kept

    def turn():
        load_trials.wait()
        beam = lax.broadcasted_iota(jnp.int32, (beams, LANES), 0)
        trial = jnp.zeros((beams, LANES), jnp.int32)
        for b in range(beams):
            trial = jnp.where(beam == b, trials[b], trial)
        scaled = (-2.0 * math.pi * DM_UNIT) * (trial.astype(jnp.float32) + 1.0)
        lane = lax.broadcasted_iota(jnp.int32, (n, beams, LANES), 2)
        owner = lax.broadcasted_iota(jnp.int32, (n, beams, LANES), 0)
        chan = (owner * locals_ + lane // half % locals_).astype(jnp.float32) / channels
        phase = scaled[None] * (chan * chan)
        chirp[0] = jnp.cos(phase)
        chirp[1] = jnp.where(lane < LANES // 2, -1.0, 1.0) * jnp.sin(phase)

    def gather_weights():
        whole(*index_args).wait_recv()
        load_weights.wait()
        lane = lax.broadcasted_iota(jnp.int32, (LANES, LANES), 1)
        lane_quad = lax.broadcasted_iota(jnp.int32, (1, LANES), 1) // antennas
        blocks = []
        for ag in range(n // quad):
            row = got_index[ag * quad]
            for q in range(1, quad):
                row = jnp.where(lane_quad == q, got_index[ag * quad + q], row)
            column = jnp.broadcast_to(row.astype(jnp.float32), (LANES, LANES)).T.astype(jnp.int32)
            blocks.append(
                jnp.concatenate(
                    [
                        jnp.where(column == lane + t * LANES, 1.0, 0.0).astype(jnp.bfloat16)
                        for t in range(WEIGHT_ROWS // LANES)
                    ],
                    1,
                )
            )
        onehot = jnp.concatenate(blocks, 0)
        for c in range(locals_):
            both = jnp.concatenate([weights[0, c], weights[1, c]], 1)
            gathered[c] = jnp.dot(onehot, both, preferred_element_type=jnp.float32).astype(jnp.bfloat16)

    load_table.wait()
    for at in range(steps):
        streams[at].wait()
        if at + 2 < steps:
            streams[at + 2].start()
        elif at + 2 == steps:
            load_weights.start()
            load_inverse.start()
        if at == 0:
            small()
        total = None
        for k in range(FORWARD_LENGTH // K_TILE):
            part = jnp.dot(
                filtered(at, k), table[k * K_TILE : (k + 1) * K_TILE, :], preferred_element_type=jnp.float32
            )
            total = part if total is None else total + part
        emit(at, total)
        if at == 0:
            pl.semaphore_wait(barrier, n - 1)
            copies(*index_args)
            got_index[me] = index_rows[0]
        copies(*piece_args(at))
    turn()
    got_spec[me] = spec[me]
    gather_weights()

    lane_part = lax.broadcasted_iota(jnp.int32, (parts, LANES), 1) // antennas

    def line(at):
        whole(*piece_args(at)).wait_recv()
        for sg in range(n // quad):
            for ft in range(*spans(at)):
                pieces = [
                    got_spec[sg * quad + s, :, ft * LANES : (ft + 1) * LANES].astype(jnp.float32)
                    for s in range(quad)
                ]
                for f in range(quad):
                    made = None
                    for s in range(quad):
                        piece = pieces[s]
                        if s != f:
                            piece = pltpu.roll(piece, ((s - f) * antennas) % LANES, 1)
                        made = piece if made is None else jnp.where(lane_part == s, piece, made)
                    to = (ft * quad + f) * parts
                    lined[sg, to : to + parts, :] = made

    def product(h):
        real, imag = [], []
        for c in range(locals_):
            left = jnp.concatenate(
                [
                    jnp.concatenate(
                        [
                            lined[sg, pl.ds(h * half * parts + r * locals_ + c, half, stride=parts), :]
                            for sg in range(n // quad)
                        ],
                        1,
                    )
                    for r in range(2)
                ],
                0,
            ).astype(jnp.bfloat16)
            both = jnp.dot(left, gathered[c], preferred_element_type=jnp.float32)
            real.append(both[:half, :beam_total] - both[half:, beam_total:])
            imag.append(both[:half, beam_total:] + both[half:, :beam_total])
        stack = jnp.concatenate(real + imag, 0)
        owners = LANES // beams
        for bt in range(beam_total // LANES):
            across = stack[:, bt * LANES : (bt + 1) * LANES].T
            sending[h, bt * owners : (bt + 1) * owners] = across.reshape(owners, beams, LANES).astype(jnp.bfloat16)

    def finish(h):
        whole(*beam_args(h)).wait_recv()
        for s in range(n):
            block = got_beams[h, s].astype(jnp.float32)
            swapped = pltpu.roll(block, LANES // 2, 1)
            turned[pl.ds(s, beams, stride=n), :] = block * chirp[0, s] + swapped * chirp[1, s]
        each = LANES // n
        deep = parts // each
        place = lax.broadcasted_iota(jnp.int32, (half, LANES), 1) // n
        for g in range(beams // each):
            across = turned[g * LANES : (g + 1) * LANES, :].T
            for b in range(each):
                for k in range(deep):
                    made = None
                    for slot in range(each):
                        piece = across[(k * each + slot) * half : (k * each + slot + 1) * half]
                        if b != slot:
                            piece = pltpu.roll(piece, ((slot - b) * n) % LANES, 1)
                        made = piece if made is None else jnp.where(place == slot, piece, made)
                    stacked[k, pl.ds(g * each + b, half, stride=beams), :] = made
        left = jnp.concatenate([stacked[k] for k in range(deep)], 1).astype(jnp.bfloat16)
        for s in range(2):
            total = jnp.dot(left, inverse[s], preferred_element_type=jnp.float32) * channels ** (-0.5)
            out[s, h * half : (h + 1) * half] = total.reshape(half, beams, channels)

    done = 0
    for h in range(halves):
        while done < steps and sum(GROUPS[:done]) < (h + 1) * half:
            line(done)
            done += 1
        product(h)
        copies(*beam_args(h))
        got_beams[h, me] = sending[h, me]
    load_inverse.wait()
    whole(*index_args).wait_send()
    for at in range(steps):
        whole(*piece_args(at)).wait_send()
    for h in range(halves):
        finish(h)
        whole(*beam_args(h)).wait_send()


def per_device(voltages, taps, weights, antenna_weight_index, flagged, trials):
    n = lax.axis_size("gx")
    locals_ = weights.shape[1]
    beam_total = weights.shape[3]
    channels = locals_ * n
    antennas = voltages.shape[0]
    beams = trials.shape[0]
    parts = 2 * locals_
    rows = 2 * channels
    half = LANES // parts
    halves = FRAME_COUNT // half
    steps = len(GROUPS)
    table = forward_columns(channels, n)
    inverse = inverse_rows(channels, n)
    room = 2 * FRAME_COUNT * beams * max(channels, LANES) * 4 + (1 << 17)
    hbm = pl.BlockSpec(memory_space=pltpu.HBM)
    return pl.pallas_call(
        functools.partial(kernel, n),
        out_shape=pltpu.VMEM((2, FRAME_COUNT, beams, channels), jnp.float32),
        in_specs=[hbm] * 8,
        out_specs=pl.BlockSpec(memory_space=pltpu.VMEM),
        scratch_shapes=[
            pltpu.SMEM(antenna_weight_index.shape, jnp.int32),
            pltpu.SMEM(flagged.shape, jnp.int32),
            pltpu.SMEM(trials.shape, jnp.int32),
            pltpu.VMEM(voltages.shape, jnp.bfloat16),
            pltpu.VMEM(taps.shape, jnp.float32),
            pltpu.VMEM(table.shape, jnp.bfloat16),
            pltpu.VMEM(weights.shape, jnp.bfloat16),
            pltpu.VMEM(inverse.shape, jnp.bfloat16),
            pltpu.VMEM((TAP_COUNT, SUBLANES, FORWARD_LENGTH), jnp.bfloat16),
            pltpu.VMEM((LANES, LANES), jnp.float32),
            pltpu.VMEM((2, n, beams, LANES), jnp.float32),
            pltpu.VMEM((n, 1, LANES), jnp.int32),
            pltpu.VMEM((n, parts, FRAME_COUNT * antennas), jnp.bfloat16),
            pltpu.VMEM((n, 1, LANES), jnp.int32),
            pltpu.VMEM((n, parts, FRAME_COUNT * antennas), jnp.bfloat16),
            pltpu.VMEM((locals_, n * antennas, 2 * beam_total), jnp.bfloat16),
            pltpu.VMEM((n * antennas // LANES, FRAME_COUNT * parts, LANES), jnp.float32),
            pltpu.VMEM((halves, n, beams, LANES), jnp.bfloat16),
            pltpu.VMEM((halves, n, beams, LANES), jnp.bfloat16),
            pltpu.VMEM((beams * n, LANES), jnp.float32),
            pltpu.VMEM((rows // LANES, half * beams, LANES), jnp.float32),
            pltpu.SemaphoreType.DMA((steps + 7,)),
            pltpu.SemaphoreType.DMA((2 * (1 + steps + halves),)),
        ],
        compiler_params=pltpu.CompilerParams(
            collective_id=0, has_side_effects=True, vmem_limit_bytes=VMEM_BYTES - room
        ),
        name="beamformer",
    )(
        antenna_weight_index, flagged, trials, voltages, taps,
        jnp.asarray(table), weights, jnp.asarray(inverse),
    )


def solution(mesh):
    return jax.shard_map(
        per_device,
        mesh=mesh,
        in_specs=(
            P(("grp", "gx"), None),
            P(),
            P(None, "gx", None, None),
            P(("grp", "gx")),
            P(("grp", "gx")),
            P(("grp", "gx")),
        ),
        out_specs=P(None, None, ("grp", "gx"), None),
        check_vma=False,
    )
```

time: 27.7 us -> 20.4 us (0.74)
  Pallas kernels: 25.9 us -> 19.5 us
  local copies, waits for them, and re-layouts: 1.67 us -> 0.71 us
    pallas_call x1, Pallas kernels: 25.9 us -> 19.5 us  [per_device(): pl.pallas_call(functools.partial(kernel, n), out_shape=pltpu.VMEM((2, FRA...]
    unnamed x1, local copies, waits for them, and re-layouts: 1.67 us -> 0.71 us
where the time goes in v1:
time: 20.4 us; the launch traced here: 20.3 us
  Pallas kernels  19.5 us (96%)
  local copies, waits for them, and re-layouts  0.71 us (3%)
    pallas_call x1, Pallas kernels, per_device(): pl.pallas_call(functools.partial(kernel, n), out_shape=pltpu.VMEM((2, FRA...  19.5 us
    unnamed x1, local copies, waits for them, and re-layouts  0.71 us

profile of v1, /device:TPU:0, one launch (start us, length us, event | category | flops | bytes accessed | tf_op | source)
XLA Modules:
  0.0 20.3 jit_solution(13085499231196027424)
XLA Ops:
  0.0 19.5 %beamformer.1 = f32[2,32,8,64]{3,2,1,0:T(8,128)S(1)} custom-call(s32[32]{0:T(128)} %index_hbm.1, s32[32]{0:T(128)} %flagged_hbm.1, s32[8]{0:T(128)} %trials_hbm.1, bf16[32,143360]{1,0:T(8,128)(2,1)} %volts_hbm.1, f32[4,4096]{1,0:T(4,128)} %taps_hbm.1, bf16[4096,128]{1,0:T(8,128)(2,1)} %constant.4.clone.table_hbm, bf16[2,4,256,128]{3,2,1,0:T(8,128)(2,1)} %weights_hbm.1, ...), custom_call_target="tpu_custom_call" | custom-call | tf_op jit(solution)/shard_map/beamformer/pallas_call | solution.py:352
  19.5 0.7 %copy.10 = f32[2,32,8,64]{3,2,1,0:T(8,128)} copy(f32[2,32,8,64]{3,2,1,0:T(8,128)S(1)} %beamformer.1) | data formatting | bytes 262144

commit v2 on v1

--- a/solution.py
+++ b/solution.py
@@ -18,18 +18,19 @@
 SUBLANES = 16
 DM_UNIT = 0.173
 MESH = pl.DeviceIdType.MESH
+NT = (((1,), (1,)), ((), ()))
 VMEM_BYTES = 67108864
 GROUPS = (8, 8, 8, 8)
 K_TILE = 256
 
 
-def forward_columns(channels, owners):
+def forward_rows(channels, owners):
     local = channels // owners
     kept = np.arange(channels).reshape(owners, 1, local)
     bins = np.broadcast_to(CH_LO + kept, (owners, 2, local)).reshape(-1)
     part = np.broadcast_to(np.arange(2).reshape(1, 2, 1), (owners, 2, local)).reshape(-1)
-    angle = (np.arange(FORWARD_LENGTH)[:, None] * bins[None] % FORWARD_LENGTH) * (2.0 * math.pi / FORWARD_LENGTH)
-    return np.where(part[None] == 0, np.cos(angle), -np.sin(angle)).astype(jnp.bfloat16)
+    angle = (bins[:, None] * np.arange(FORWARD_LENGTH)[None] % FORWARD_LENGTH) * (2.0 * math.pi / FORWARD_LENGTH)
+    return np.where(part[:, None] == 0, np.cos(angle), -np.sin(angle)).astype(jnp.bfloat16)
 
 
 def inverse_rows(channels, owners):
@@ -46,10 +47,12 @@
     n, index_hbm, flagged_hbm, trials_hbm, volts_hbm, taps_hbm, table_hbm, weights_hbm, inverse_hbm, out,
     index, flagged, trials, volts, taps, table, weights, inverse,
     wide_taps, keep, chirp, index_rows, spec,
-    got_index, got_spec, gathered, lined, sending, got_beams, turned, stacked,
-    load_sems, remote_sems,
+    got_index, got_spec, gathered, partial, lined, sending, got_beams, turned,
+    load_sems, remote_sems, spec_sems,
 ):
     me = lax.axis_index("gx")
+    mine = me // (n // 2)
+    yours = 1 - mine
     antennas = volts.shape[0]
     locals_ = weights.shape[1]
     beam_total = weights.shape[3]
@@ -85,11 +88,12 @@
     load_trials = load(trials_hbm, trials, steps + 6)
     for one in (load_taps, load_table, streams[0], load_index, load_flagged, load_trials):
         one.start()
-    streams[1].start()
+    for one in streams[1:] + [load_weights, load_inverse]:
+        one.start()
+    peers = [lax.rem(me + d, n) for d in range(n)]
 
     def copies(source, target, send, recv):
-        for d in range(1, n):
-            peer = lax.rem(me + d, n)
+        for peer in peers[1:]:
             pltpu.make_async_remote_copy(
                 src_ref=source(peer),
                 dst_ref=target(me),
@@ -99,8 +103,8 @@
                 device_id_type=MESH,
             ).start()
 
-    def whole(source, target, send, recv):
-        others = pl.ds(0, n - 1)
+    def whole(source, target, send, recv, count=n - 1):
+        others = pl.ds(0, count)
         return pltpu.make_async_remote_copy(
             src_ref=source(others),
             dst_ref=target(others),
@@ -115,18 +119,18 @@
     def spans(at):
         return sum(GROUPS[:at]) // quad, sum(GROUPS[: at + 1]) // quad
 
-    def piece_args(at):
+    def piece_args(at, side):
         first, last = spans(at)
         span = pl.ds(first * LANES, (last - first) * LANES)
         return (
             lambda p: spec.at[p, :, span], lambda p: got_spec.at[p, :, span],
-            remote_sems.at[2 + 2 * at], remote_sems.at[3 + 2 * at],
+            remote_sems.at[2], spec_sems.at[at, side],
         )
 
     def beam_args(h):
         return (
             lambda p: sending.at[h, p], lambda p: got_beams.at[h, p],
-            remote_sems.at[2 + 2 * (steps + h)], remote_sems.at[3 + 2 * (steps + h)],
+            remote_sems.at[3], remote_sems.at[4 + h],
         )
 
     load_taps.wait()
@@ -156,14 +160,10 @@
 
     def emit(at, total):
         first, last = spans(at)
-        eights = LANES // parts
-        for tile in range(first, last):
-            block = total[(tile - first) * LANES : (tile - first + 1) * LANES]
-            for part in range(rows // LANES):
-                across = (block[:, part * LANES : (part + 1) * LANES] * keep[...]).T
-                spec[part * eights : (part + 1) * eights, :, tile * LANES : (tile + 1) * LANES] = across.reshape(
-                    eights, parts, LANES
-                ).astype(jnp.bfloat16)
+        kept = jnp.concatenate([keep[...]] * (last - first), 1)
+        spec[:, :, first * LANES : last * LANES] = (total * kept).reshape(n, parts, (last - first) * LANES).astype(
+            jnp.bfloat16
+        )
 
     def small():
         load_index.wait()
@@ -173,13 +173,10 @@
         for a in range(antennas):
             row = jnp.where(lane_one == a, index[a], row)
         index_rows[...] = jnp.broadcast_to(row[None], index_rows.shape)
-        antenna = lax.broadcasted_iota(jnp.int32, (antennas, LANES), 0)
-        off = jnp.zeros((antennas, LANES), jnp.int32)
+        off = jnp.zeros((1, LANES), jnp.int32)
         for a in range(antennas):
-            off = jnp.where(antenna == a, flagged[a], off)
-        kept = (1 - off).astype(jnp.float32) * FORWARD_LENGTH ** (-0.5)
-        for q in range(quad):
-            keep[q * antennas : (q + 1) * antennas, :] = kept
+            off = jnp.where(lane_one == a, flagged[a], off)
+        keep[...] = (1 - off).astype(jnp.float32) * FORWARD_LENGTH ** (-0.5)
 
     def turn():
         load_trials.wait()
@@ -223,34 +220,40 @@
     load_table.wait()
     for at in range(steps):
         streams[at].wait()
-        if at + 2 < steps:
-            streams[at + 2].start()
-        elif at + 2 == steps:
-            load_weights.start()
-            load_inverse.start()
         if at == 0:
             small()
-        total = None
+        sums = [None, None]
         for k in range(FORWARD_LENGTH // K_TILE):
-            part = jnp.dot(
-                filtered(at, k), table[k * K_TILE : (k + 1) * K_TILE, :], preferred_element_type=jnp.float32
-            )
-            total = part if total is None else total + part
+            y = filtered(at, k)
+            middle = y.shape[0] // 2
+            for i in range(2):
+                part = lax.dot_general(
+                    table[:, k * K_TILE : (k + 1) * K_TILE], y[i * middle : (i + 1) * middle], NT,
+                    preferred_element_type=jnp.float32,
+                )
+                sums[i] = part if sums[i] is None else sums[i] + part
+        total = jnp.concatenate(sums, 1)
         emit(at, total)
-        if at == 0:
-            pl.semaphore_wait(barrier, n - 1)
-            copies(*index_args)
-            got_index[me] = index_rows[0]
-        copies(*piece_args(at))
+
+        @pl.when(me >= 0)
+        def _():
+            if at == 0:
+                pl.semaphore_wait(barrier, n - 1)
+                copies(*index_args)
+                got_index[me] = index_rows[0]
+            copies(*piece_args(at, mine))
+
     turn()
     got_spec[me] = spec[me]
     gather_weights()
 
     lane_part = lax.broadcasted_iota(jnp.int32, (parts, LANES), 1) // antennas
 
-    def line(at):
-        whole(*piece_args(at)).wait_recv()
-        for sg in range(n // quad):
+    def line(at, side):
+        count = n // 2 if side is yours else n // 2 - 1
+        whole(*piece_args(at, side), count).wait_recv()
+        planes = n // quad // 2
+        for sg in [side * planes + i for i in range(planes)]:
             for ft in range(*spans(at)):
                 pieces = [
                     got_spec[sg * quad + s, :, ft * LANES : (ft + 1) * LANES].astype(jnp.float32)
@@ -266,15 +269,17 @@
                     to = (ft * quad + f) * parts
                     lined[sg, to : to + parts, :] = made
 
-    def product(h):
-        real, imag = [], []
+    def product(h, side):
+        planes = n // quad // 2
+        deep = planes * LANES
+        made = []
         for c in range(locals_):
             left = jnp.concatenate(
                 [
                     jnp.concatenate(
                         [
-                            lined[sg, pl.ds(h * half * parts + r * locals_ + c, half, stride=parts), :]
-                            for sg in range(n // quad)
+                            lined[side * planes + i, pl.ds(h * half * parts + r * locals_ + c, half, stride=parts), :]
+                            for i in range(planes)
                         ],
                         1,
                     )
@@ -282,9 +287,13 @@
                 ],
                 0,
             ).astype(jnp.bfloat16)
-            both = jnp.dot(left, gathered[c], preferred_element_type=jnp.float32)
-            real.append(both[:half, :beam_total] - both[half:, beam_total:])
-            imag.append(both[:half, beam_total:] + both[half:, :beam_total])
+            right = gathered[c, pl.ds(pl.multiple_of(side * deep, deep), deep), :]
+            made.append(jnp.dot(left, right, preferred_element_type=jnp.float32))
+        return made
+
+    def spread(h, made):
+        real = [both[:half, :beam_total] - both[half:, beam_total:] for both in made]
+        imag = [both[:half, beam_total:] + both[half:, :beam_total] for both in made]
         stack = jnp.concatenate(real + imag, 0)
         owners = LANES // beams
         for bt in range(beam_total // LANES):
@@ -300,37 +309,51 @@
         each = LANES // n
         deep = parts // each
         place = lax.broadcasted_iota(jnp.int32, (half, LANES), 1) // n
+        masks = [jnp.where(place == slot, 1.0, 0.0).astype(jnp.bfloat16) for slot in range(each)]
+        left = []
         for g in range(beams // each):
-            across = turned[g * LANES : (g + 1) * LANES, :].T
+            across = turned[g * LANES : (g + 1) * LANES, :].T.astype(jnp.bfloat16)
             for b in range(each):
+                tiles = []
                 for k in range(deep):
                     made = None
                     for slot in range(each):
                         piece = across[(k * each + slot) * half : (k * each + slot + 1) * half]
                         if b != slot:
                             piece = pltpu.roll(piece, ((slot - b) * n) % LANES, 1)
-                        made = piece if made is None else jnp.where(place == slot, piece, made)
-                    stacked[k, pl.ds(g * each + b, half, stride=beams), :] = made
-        left = jnp.concatenate([stacked[k] for k in range(deep)], 1).astype(jnp.bfloat16)
+                        piece = piece * masks[slot]
+                        made = piece if made is None else made + piece
+                    tiles.append(made)
+                left.append(jnp.concatenate(tiles, 1))
+        left = jnp.concatenate(left, 0)
         for s in range(2):
             total = jnp.dot(left, inverse[s], preferred_element_type=jnp.float32) * channels ** (-0.5)
-            out[s, h * half : (h + 1) * half] = total.reshape(half, beams, channels)
+            for b in range(beams):
+                out[s, h * half : (h + 1) * half, b, :] = total[b * half : (b + 1) * half]
 
     done = 0
     for h in range(halves):
-        while done < steps and sum(GROUPS[:done]) < (h + 1) * half:
-            line(done)
+        while sum(GROUPS[: done + 1]) < (h + 1) * half:
+            line(done, mine)
+            line(done, yours)
             done += 1
-        product(h)
+        line(done, mine)
+        for c, both in enumerate(product(h, mine)):
+            partial[c] = both
+        line(done, yours)
+        far = product(h, yours)
+        done += 1
+        spread(h, [partial[c] + both for c, both in enumerate(far)])
         copies(*beam_args(h))
         got_beams[h, me] = sending[h, me]
     load_inverse.wait()
     whole(*index_args).wait_send()
-    for at in range(steps):
-        whole(*piece_args(at)).wait_send()
+    whole(lambda p: spec.at[p], lambda p: got_spec.at[p], remote_sems.at[2], remote_sems.at[1]).wait_send()
     for h in range(halves):
         finish(h)
-        whole(*beam_args(h)).wait_send()
+    whole(
+        lambda p: sending.at[:, p], lambda p: got_beams.at[:, p], remote_sems.at[3], remote_sems.at[4]
+    ).wait_send()
 
 
 def per_device(voltages, taps, weights, antenna_weight_index, flagged, trials):
@@ -345,7 +368,7 @@
     half = LANES // parts
     halves = FRAME_COUNT // half
     steps = len(GROUPS)
-    table = forward_columns(channels, n)
+    table = forward_rows(channels, n)
     inverse = inverse_rows(channels, n)
     room = 2 * FRAME_COUNT * beams * max(channels, LANES) * 4 + (1 << 17)
     hbm = pl.BlockSpec(memory_space=pltpu.HBM)
@@ -364,20 +387,21 @@
             pltpu.VMEM(weights.shape, jnp.bfloat16),
             pltpu.VMEM(inverse.shape, jnp.bfloat16),
             pltpu.VMEM((TAP_COUNT, SUBLANES, FORWARD_LENGTH), jnp.bfloat16),
-            pltpu.VMEM((LANES, LANES), jnp.float32),
+            pltpu.VMEM((1, LANES), jnp.float32),
             pltpu.VMEM((2, n, beams, LANES), jnp.float32),
             pltpu.VMEM((n, 1, LANES), jnp.int32),
             pltpu.VMEM((n, parts, FRAME_COUNT * antennas), jnp.bfloat16),
             pltpu.VMEM((n, 1, LANES), jnp.int32),
             pltpu.VMEM((n, parts, FRAME_COUNT * antennas), jnp.bfloat16),
             pltpu.VMEM((locals_, n * antennas, 2 * beam_total), jnp.bfloat16),
+            pltpu.VMEM((locals_, 2 * half, 2 * beam_total), jnp.float32),
             pltpu.VMEM((n * antennas // LANES, FRAME_COUNT * parts, LANES), jnp.float32),
             pltpu.VMEM((halves, n, beams, LANES), jnp.bfloat16),
             pltpu.VMEM((halves, n, beams, LANES), jnp.bfloat16),
             pltpu.VMEM((beams * n, LANES), jnp.float32),
-            pltpu.VMEM((rows // LANES, half * beams, LANES), jnp.float32),
             pltpu.SemaphoreType.DMA((steps + 7,)),
-            pltpu.SemaphoreType.DMA((2 * (1 + steps + halves),)),
+            pltpu.SemaphoreType.DMA((4 + halves,)),
+            pltpu.SemaphoreType.DMA((steps, 2)),
         ],
         compiler_params=pltpu.CompilerParams(
             collective_id=0, has_side_effects=True, vmem_limit_bytes=VMEM_BYTES - room

time: 20.4 us -> 20.3 us (level)
  no operation moved by 1% of the time
where the time goes in v2:
time: 20.3 us; the launch traced here: 20.1 us
  Pallas kernels  19.4 us (96%)
  local copies, waits for them, and re-layouts  0.71 us (3%)
    pallas_call x1, Pallas kernels, per_device(): pl.pallas_call(functools.partial(kernel, n), out_shape=pltpu.VMEM((2, FRA...  19.4 us
    unnamed x1, local copies, waits for them, and re-layouts  0.71 us

profile of v2, /device:TPU:0, one launch (start us, length us, event | category | flops | bytes accessed | tf_op | source)
XLA Modules:
  0.0 20.1 jit_solution(8449291072044051598)
XLA Ops:
  0.0 19.4 %beamformer.1 = f32[2,32,8,64]{3,2,1,0:T(8,128)S(1)} custom-call(s32[32]{0:T(128)} %index_hbm.1, s32[32]{0:T(128)} %flagged_hbm.1, s32[8]{0:T(128)} %trials_hbm.1, bf16[32,143360]{1,0:T(8,128)(2,1)} %volts_hbm.1, f32[4,4096]{1,0:T(4,128)} %taps_hbm.1, bf16[128,4096]{1,0:T(8,128)(2,1)} %constant.4.clone.table_hbm, bf16[2,4,256,128]{3,2,1,0:T(8,128)(2,1)} %weights_hbm.1, ...), custom_call_target="tpu_custom_call" | custom-call | tf_op jit(solution)/shard_map/beamformer/pallas_call | solution.py:375
  19.4 0.7 %copy.10 = f32[2,32,8,64]{3,2,1,0:T(8,128)} copy(f32[2,32,8,64]{3,2,1,0:T(8,128)S(1)} %beamformer.1) | data formatting | bytes 262144

commit v3 on v2

--- a/solution.py
+++ b/solution.py
@@ -22,6 +22,7 @@
 VMEM_BYTES = 67108864
 GROUPS = (8, 8, 8, 8)
 K_TILE = 256
+LATE = 1
 
 
 def forward_rows(channels, owners):
@@ -66,6 +67,7 @@
     beams = beam_total // n
     steps = len(GROUPS)
 
+    enter = LATE * (1 - lax.min(me // (3 * n // 8), 1))
     barrier = pltpu.get_barrier_semaphore()
     for d in range(1, n):
         pl.semaphore_signal(barrier, inc=1, device_id={"gx": lax.rem(me + d, n)}, device_id_type=MESH)
@@ -235,12 +237,17 @@
         total = jnp.concatenate(sums, 1)
         emit(at, total)
 
-        @pl.when(me >= 0)
-        def _():
-            if at == 0:
+        if at in (0, LATE):
+            @pl.when(enter == at)
+            def _():
                 pl.semaphore_wait(barrier, n - 1)
                 copies(*index_args)
                 got_index[me] = index_rows[0]
+                for earlier in range(at):
+                    copies(*piece_args(earlier, mine))
+
+        @pl.when(enter <= at)
+        def _():
             copies(*piece_args(at, mine))
 
     turn()

time: 20.3 us -> 20.3 us (level)
  no operation moved by 1% of the time
where the time goes in v3:
time: 20.3 us; the launch traced here: 20.2 us
  Pallas kernels  19.5 us (96%)
  local copies, waits for them, and re-layouts  0.71 us (3%)
    pallas_call x1, Pallas kernels, per_device(): pl.pallas_call(functools.partial(kernel, n), out_shape=pltpu.VMEM((2, FRA...  19.5 us
    unnamed x1, local copies, waits for them, and re-layouts  0.71 us

profile of v3, /device:TPU:0, one launch (start us, length us, event | category | flops | bytes accessed | tf_op | source)
XLA Modules:
  0.0 20.2 jit_solution(14874883731672541596)
XLA Ops:
  0.0 19.5 %beamformer.1 = f32[2,32,8,64]{3,2,1,0:T(8,128)S(1)} custom-call(s32[32]{0:T(128)} %index_hbm.1, s32[32]{0:T(128)} %flagged_hbm.1, s32[8]{0:T(128)} %trials_hbm.1, bf16[32,143360]{1,0:T(8,128)(2,1)} %volts_hbm.1, f32[4,4096]{1,0:T(4,128)} %taps_hbm.1, bf16[128,4096]{1,0:T(8,128)(2,1)} %constant.4.clone.table_hbm, bf16[2,4,256,128]{3,2,1,0:T(8,128)(2,1)} %weights_hbm.1, ...), custom_call_target="tpu_custom_call" | custom-call | tf_op jit(solution)/shard_map/beamformer/pallas_call | solution.py:382
  19.5 0.7 %copy.10 = f32[2,32,8,64]{3,2,1,0:T(8,128)} copy(f32[2,32,8,64]{3,2,1,0:T(8,128)S(1)} %beamformer.1) | data formatting | bytes 262144
